TPU v7x, 256 devices: a whole 4x4x8 slice. The times are simulated.
256 devices in a mesh: dp: 32 (over z_lo, x, core), mp: 8 (over z_hi, y).
Axes of the slice: x: 4, y: 4, z: 8 (z_hi: 2, z_lo: 4; z = z_hi * 4 + z_lo), core: 2. Of those that a mesh axis runs over, the one named last changes fastest.
Arguments:
- clean: bfloat16 [32, 1024, 1280], P('dp', 'mp'), may hold values from -6 to 6
- noise: bfloat16 [32, 1024, 1280], P('dp', 'mp'), may hold values from -6 to 6
- tsteps: int32 [32], P('dp'), may hold values from 0 to 999
- alpha_tab: float32 [1000], replicated, may hold values from 0.3 to 0.99
- weight_tab: float32 [1000], replicated, may hold values from 0.1 to 3
- norm1_gain: float32 [1280], replicated, may hold values from 0.1 to 1.9
- norm2_gain: float32 [1280], replicated, may hold values from 0.1 to 1.9
- wqkv: bfloat16 [3, 1280, 1280], P(None, 'dp', 'mp'), may hold values from -4 to 4
- wout: bfloat16 [1280, 1280], P('dp', 'mp'), may hold values from -0.625 to 0.625
- wgate: bfloat16 [1280, 5120], P('dp', 'mp'), may hold values from -0.15625 to 0.15625
- wvalue: bfloat16 [1280, 5120], P('dp', 'mp'), may hold values from -0.15625 to 0.15625
- wdown: bfloat16 [5120, 1280], P('mp', 'dp'), may hold values from -0.078125 to 0.078125
Outputs:
- denoised: float32 [32, 1024, 1280], P('dp', 'mp')
- loss: float32 [], replicated
All inputs are finite; a program needn't handle non-finite values.
Results may differ from a plain program's by a relative error of at most 0.02.
Values may be sent and summed in bfloat16 or wider, within the bound.
A program may use at most 64 MiB of HBM per device.

v0:
```python
import jax
import jax.numpy as jnp
from jax import lax
from jax.sharding import Mesh
from jax.sharding import PartitionSpec as P

D = 1280
HEADS = 20
HEAD = 64
L = 1024
MP = ("mp_0", "mp_1")
DP = ("dp_0", "dp_1", "dp_2")
DP_MP = ("dp_0", "dp_1", "dp_2", "mp_0", "mp_1")


def copy_for_each(value, axis):
    length = lax.axis_size(axis)
    return lax.all_to_all(
        jnp.broadcast_to(value[None], (length, *value.shape)), axis, 0, 0, tiled=True
    )


def in_order(blocks, dim):
    blocks = jnp.moveaxis(blocks, 0, dim)
    dims = blocks.shape
    return blocks.reshape(*dims[:dim], dims[dim] * dims[dim + 1], *dims[dim + 2 :])


def gathered_copies(value, axis, dim):
    blocks = copy_for_each(value, axis)
    return in_order(blocks, dim)


def sent_together(arrays, axis, dim, along):
    ends, at = ([], 0)
    for a in arrays[:-1]:
        at += a.shape[along]
        ends.append(at)
    both = jnp.concatenate(arrays, axis=along)
    return tuple(jnp.split(lax.all_gather(both, axis, axis=dim, tiled=True), ends, axis=along))


def whole_of(value, axes, dim):
    far, near = axes
    blocks = copy_for_each(copy_for_each(value, far), near)
    return in_order(blocks.swapaxes(0, 1).reshape(-1, *value.shape), dim)


def sum_in_order(blocks, axes, order):
    inside = blocks.shape[1:]
    blocks = blocks.reshape(*(lax.axis_size(a) for a in axes), *inside)
    blocks = jnp.moveaxis(blocks, order, range(len(axes))).reshape(-1, *inside)
    for k in order:
        blocks = lax.psum_scatter(blocks, axes[k], scatter_dimension=0, tiled=True)
    return blocks[0]


def in_blocks(value, dim, length):
    before, after = (value.shape[:dim], value.shape[dim + 1 :])
    return jnp.moveaxis(value.reshape(*before, length, -1, *after), dim, 0)


def sum_by_axis(value, axes, order, dim):
    length = lax.axis_size(axes)
    return sum_in_order(in_blocks(value, dim, length), axes, order)


def by_axis(value, axes):
    for axis in axes:
        value = lax.psum(value, axis)
    return value


def lookup(steps, table):
    match = steps[:, None] == jnp.arange(table.shape[0], dtype=jnp.int32)[None, :]
    return jnp.sum(jnp.where(match, table[None, :], jnp.zeros((), table.dtype)), axis=1)


def layer_norm(values, gain):
    wide = values.astype(jnp.float32)
    center = wide - jnp.mean(wide, axis=-1, keepdims=True)
    spread = jnp.mean(center * center, axis=-1, keepdims=True)
    return (center * lax.rsqrt(spread + 1e-05) * gain).astype(jnp.bfloat16)


def make_adder(flat, piece):
    return jnp.einsum("rn,tnc->trc", flat, piece, preferred_element_type=jnp.float32)


def attend(operands):
    query_one, keys_one, values_one = operands
    rows = query_one.shape[0]
    total = keys_one.shape[0]
    scores = jnp.einsum(
        "qhd,khd->hqk",
        query_one.reshape(rows, HEADS, HEAD),
        keys_one.reshape(total, HEADS, HEAD),
        preferred_element_type=jnp.float32,
    ) * HEAD ** (-0.5)
    probs = jax.nn.softmax(scores, axis=-1).astype(jnp.bfloat16)
    mixed = jnp.einsum(
        "hqk,khd->qhd",
        probs,
        values_one.reshape(total, HEADS, HEAD),
        preferred_element_type=jnp.float32,
    )
    return mixed.astype(jnp.bfloat16).reshape(rows, D)


def shards(
    clean,
    noise,
    tsteps,
    alpha_tab,
    weight_tab,
    norm1_gain,
    norm2_gain,
    wqkv,
    wout,
    wgate,
    wvalue,
    wdown,
):
    samples, local_rows, width = clean.shape
    alpha = lookup(tsteps, alpha_tab)
    sigma = jnp.sqrt(1.0 - alpha * alpha)
    weight = lookup(tsteps, weight_tab)
    noised = (
        alpha[:, None, None] * clean.astype(jnp.float32)
        + sigma[:, None, None] * noise.astype(jnp.float32)
    ).astype(jnp.bfloat16)
    normed1 = layer_norm(noised, norm1_gain)
    full_cols = gathered_copies(wqkv, MP, 2)
    flat = normed1.reshape(samples * local_rows, width)
    projected = make_adder(flat, lax.all_gather(full_cols, DP, axis=1, tiled=True)).astype(
        jnp.bfloat16
    )
    query = projected[0].reshape(samples, local_rows, width)
    keys_part = projected[1].reshape(samples, local_rows, width)
    values_part = projected[2].reshape(samples, local_rows, width)
    keys_all, values_all = sent_together((keys_part, values_part), MP, 1, 0)
    mixed = lax.map(attend, (query, keys_all, values_all))
    mixed_flat = mixed.reshape(samples * local_rows, width)
    out_cols = gathered_copies(wout, MP, 1)
    part = mixed_flat
    projected_out = jnp.dot(
        part, whole_of(out_cols, (("dp_0", "dp_1"), "dp_2"), 0), preferred_element_type=jnp.float32
    )
    resid = (noised.astype(jnp.float32) + projected_out.reshape(samples, local_rows, width)).astype(
        jnp.bfloat16
    )
    normed2 = layer_norm(resid, norm2_gain)
    ff_in = lax.all_gather(normed2, MP, axis=1, tiled=True)
    all_rows = ff_in.shape[1]
    ff_flat = ff_in.reshape(samples * all_rows, width)
    pieces = sent_together((wgate, wvalue), DP, 0, 1)
    part = ff_flat
    gate = jnp.dot(part, pieces[0], preferred_element_type=jnp.float32)
    value = jnp.dot(part, pieces[1], preferred_element_type=jnp.float32)
    hidden = (jax.nn.gelu(gate, approximate=False) * value).astype(jnp.bfloat16)
    block_sum = jnp.dot(
        hidden, whole_of(wdown, (("dp_0", "dp_1"), "dp_2"), 1), preferred_element_type=jnp.float32
    )
    ff_out = sum_by_axis(
        block_sum.reshape(samples, all_rows, width).astype(jnp.bfloat16), MP, (1, 0), 1
    ).astype(jnp.float32)
    prediction = resid.astype(jnp.float32) + ff_out
    denoised = (noised.astype(jnp.float32) - sigma[:, None, None] * prediction) / alpha[
        :, None, None
    ]
    error = denoised - clean.astype(jnp.float32)
    local_terms = jnp.sum(weight * jnp.sum(error * error, axis=(1, 2))) / (L * D)
    loss = by_axis(local_terms, DP_MP)
    return (denoised, loss)


def solution(mesh):
    split = Mesh(mesh.devices.reshape(4, 4, 2, 2, 4), ("dp_0", "dp_1", "dp_2", "mp_0", "mp_1"))
    in_specs = (
        P(DP, MP, None),
        P(DP, MP, None),
        P(DP),
        P(),
        P(),
        P(),
        P(),
        P(None, DP, MP),
        P(DP, MP),
        P(DP, MP),
        P(DP, MP),
        P(MP, DP),
    )
    out_specs = (P(DP, MP, None), P())
    return jax.shard_map(
        shards, mesh=split, in_specs=in_specs, out_specs=out_specs, check_vma=False
    )
```

profile of v0, /device:TPU:32, one launch (start us, length us, event | category | flops | bytes accessed | tf_op | source)
XLA Modules:
  0.0 535.7 jit_solution(18051994592071202623)
XLA Ops:
  7.3 0.9 broadcast_in_dim.27
  8.2 28.9 %all_to_all.30 = bf16[8,3,40,160]{3,2,1,0:T(8,128)(2,1)S(1)} all-to-all(bf16[8,3,40,160]{3,2,1,0:T(8,128)(2,1)S(1)} %broadcast_in_dim.27), channel_id=1, replica_groups=mesh['dp_0'=4,'dp_1'=4,'dp_2'=2,'mp_0'=2,'mp_1'=4] {'mp_0','mp_1'}, dimensions={0} | all-to-all | bytes 614400 | tf_op jit(solution)/shard_map/all_to_all | solution.py:18
  37.2 1.2 reshape.152
  42.0 62.0 %all-gather.5.cloned.1.call-done = bf16[3,1280,1280]{2,1,0:T(8,128)(2,1)} async-done(((bf16[3,40,1280]{2,1,0:T(8,128)(2,1)}), bf16[3,1280,1280]{2,1,0:T(8,128)(2,1)}) %all-gather.5.cloned.1.call-update) | async-done | bytes 9830416 | tf_op jit(solution)/shard_map/all_gather | solution.py:135
  104.0 5.3 fusion.21
  110.2 20.1 %all_to_all.31 = bf16[8,40,160]{2,1,0:T(8,128)(2,1)S(1)} all-to-all(bf16[8,40,160]{2,1,0:T(8,128)(2,1)S(1)} %broadcast_in_dim.28), channel_id=1, replica_groups=mesh['dp_0'=4,'dp_1'=4,'dp_2'=2,'mp_0'=2,'mp_1'=4] {'mp_0','mp_1'}, dimensions={0} | all-to-all | bytes 204800 | tf_op jit(solution)/shard_map/all_to_all | solution.py:18
  130.6 1.3 broadcast_in_dim.30
  131.9 5.5 %all-to-all-start.2 = ((bf16[16,40,1280]{2,1,0:T(8,128)(2,1)}), bf16[16,40,1280]{2,1,0:T(8,128)(2,1)S(1)}, u32[]{:S(2)}, u32[]{:S(2)}) async-start(bf16[16,40,1280]{2,1,0:T(8,128)(2,1)} %broadcast_in_dim.30), calls=%async_computation.2 | async-start | bytes 3276800 | tf_op jit(solution)/shard_map/all_to_all | solution.py:18
  138.2 94.0 %all-to-all-done.2 = bf16[16,40,1280]{2,1,0:T(8,128)(2,1)S(1)} async-done(((bf16[16,40,1280]{2,1,0:T(8,128)(2,1)}), bf16[16,40,1280]{2,1,0:T(8,128)(2,1)S(1)}, u32[]{:S(2)}, u32[]{:S(2)}) %all-to-all-start.2) | async-done | bytes 1638432 | tf_op jit(solution)/shard_map/all_to_all | solution.py:18
  232.4 6.4 %all_to_all.32 = bf16[2,16,40,1280]{3,2,1,0:T(8,128)(2,1)S(1)} all-to-all(bf16[2,16,40,1280]{3,2,1,0:T(8,128)(2,1)S(1)} %broadcast_in_dim.31), channel_id=1, replica_groups=mesh['dp_0'=4,'dp_1'=4,'dp_2'=2,'mp_0'=2,'mp_1'=4] {'dp_2'}, dimensions={0} | all-to-all | bytes 6553600 | tf_op jit(solution)/shard_map/all_to_all | solution.py:18
  238.8 1.9 copy.28
  240.7 0.9 copy.25
  241.6 4.4 fusion.88
  246.0 4.5 copy.24
  250.5 2.7 copy.26
  253.2 9.2 %fusion.89 = (f32[20,128]{1,0:T(8,128)S(1)}, f32[20,128,1024]{2,1,0:T(8,128)}) fusion(bf16[128,20,64]{0,2,1:T(8,128)(2,1)} %bitcast.72, bf16[1024,20,64]{0,2,1:T(8,128)(2,1)} %bitcast.66), kind=kOutput, calls=%fused_computation.105 | convolution fusion | flops 343409664 | bytes 13445120 | tf_op jit(solution)/shard_map/while/body/eval_jaxpr/sub | solution.py:100
  262.4 6.2 %fusion.28 = bf16[20,64,128]{2,1,0:T(8,128)(2,1)S(1)} fusion(bf16[1024,20,64]{0,2,1:T(8,128)(2,1)S(1)} %bitcast.65, f32[20,128,1024]{2,1,0:T(8,128)} %get-tuple-element.24, f32[20,128]{1,0:T(8,128)S(1)} %get-tuple-element.23), kind=kOutput, calls=%fused_computation.40 | convolution fusion | flops 340951040 | bytes 13445120 | tf_op jit(solution)/shard_map/while/body/eval_jaxpr/hqk,khd->qhd/dot_general | solution.py:101
  269.7 0.9 multiply_convert_fusion
  270.7 30.8 %all_to_all.33 = bf16[16,640,40]{1,2,0:T(8,128)(2,1)S(1)} all-to-all(bf16[16,640,40]{1,2,0:T(8,128)(2,1)S(1)} %broadcast_in_dim.32), channel_id=1, replica_groups=mesh['dp_0'=4,'dp_1'=4,'dp_2'=2,'mp_0'=2,'mp_1'=4] {'dp_0','dp_1'}, dimensions={0} | all-to-all | bytes 1638400 | tf_op jit(solution)/shard_map/all_to_all | solution.py:18
  301.6 5.1 all_to_all.34
  306.8 83.4 %all-gather.9.cloned.1.call-done = bf16[1,1024,1280]{2,1,0:T(8,128)(2,1)} async-done(((bf16[1,128,1280]{2,1,0:T(8,128)(2,1)}), bf16[1,1024,1280]{2,1,0:T(8,128)(2,1)}) %all-gather.9.cloned.1.call-update) | async-done | bytes 2621456 | tf_op jit(solution)/shard_map/all_gather | solution.py:153
  390.2 5.9 %fusion.10 = f32[1024,640]{1,0:T(8,128)} fusion(bf16[1,1024,1280]{2,1,0:T(8,128)(2,1)} %all-gather.9.cloned.1.call-done, bf16[1280,1280]{1,0:T(8,128)(2,1)} %all-gather.11.cloned.1.call-done), kind=kOutput, calls=%fused_computation.14 | convolution fusion | flops 1677721600 | bytes 6881280 | tf_op jit(solution)/shard_map/dot_general | solution.py:159
  396.2 12.9 %convolution_convert_fusion = bf16[1024,1280]{1,0:T(8,128)(2,1)} fusion(bf16[640,1280]{0,1:T(8,128)(2,1)S(1)} %bitcast.69, f32[1024,640]{1,0:T(8,128)} %fusion.10, bf16[1,1024,1280]{2,1,0:T(8,128)(2,1)} %all-gather.9.cloned.1.call-done, bf16[1280,1280]{1,0:T(8,128)(2,1)} %all-gather.11.cloned.1.call-done), kind=kOutput, calls=%fused_computation.8 | convolution fusion | flops 3400007680 | bytes 11141120 | tf_op jit(solution)/shard_map/dot_general | solution.py:161
  409.1 3.4 copy.30
  412.6 33.2 %reduce-scatter.3.cloned.1.call-done = bf16[2,1,128,1280]{3,2,1,0:T(8,128)(2,1)} async-done(((bf16[8,1,128,1280]{3,2,1,0:T(8,128)(2,1)}), bf16[2,1,128,1280]{3,2,1,0:T(8,128)(2,1)}) %reduce-scatter.3.cloned.1.call-update) | async-done | bytes 655376 | tf_op jit(solution)/shard_map/reduce_scatter | solution.py:54
  446.5 33.0 %reduce-scatter.5.cloned.1.call-done = bf16[1,1,128,1280]{3,2,1,0:T(8,128)(2,1)} async-done(((bf16[2,1,128,1280]{3,2,1,0:T(8,128)(2,1)}), bf16[1,1,128,1280]{3,2,1,0:T(8,128)(2,1)}) %reduce-scatter.5.cloned.1.call-update) | async-done | bytes 327696 | tf_op jit(solution)/shard_map/reduce_scatter | solution.py:54
  479.5 3.2 fusion.47
  484.0 10.2 %psum.35 = f32[]{:T(128)} all-reduce(f32[]{:T(128)S(6)} %div.40), channel_id=1, replica_groups=mesh['dp_0'=4,'dp_1'=4,'dp_2'=2,'mp_0'=2,'mp_1'=4] {'dp_0'}, use_global_device_ids=true, to_apply=%region_11.12 | all-reduce | flops 1 | bytes 8 | tf_op jit(solution)/shard_map/psum | solution.py:70
  494.2 11.1 %psum.36 = f32[]{:T(128)} all-reduce(f32[]{:T(128)} %psum.35), channel_id=1, replica_groups=mesh['dp_0'=4,'dp_1'=4,'dp_2'=2,'mp_0'=2,'mp_1'=4] {'dp_1'}, use_global_device_ids=true, to_apply=%region_12.13 | all-reduce | flops 1 | bytes 8 | tf_op jit(solution)/shard_map/psum | solution.py:70
  505.2 3.1 psum.37
  508.3 9.4 %psum.38 = f32[]{:T(128)} all-reduce(f32[]{:T(128)} %psum.37), channel_id=1, replica_groups=mesh['dp_0'=4,'dp_1'=4,'dp_2'=2,'mp_0'=2,'mp_1'=4] {'mp_0'}, use_global_device_ids=true, to_apply=%region_14.15 | all-reduce | flops 1 | bytes 8 | tf_op jit(solution)/shard_map/psum | solution.py:70
  517.8 11.1 %psum.39 = f32[]{:T(128)} all-reduce(f32[]{:T(128)} %psum.38), channel_id=1, replica_groups=mesh['dp_0'=4,'dp_1'=4,'dp_2'=2,'mp_0'=2,'mp_1'=4] {'mp_1'}, use_global_device_ids=true, to_apply=%region_15.16 | all-reduce | flops 1 | bytes 8 | tf_op jit(solution)/shard_map/psum | solution.py:70
  (59 shorter events, 6.1 us)
Async XLA Ops:
  7.2 31.9 %copy-start.10 = (f32[1000]{0:T(1024)S(1)}, f32[1000]{0:T(1024)}, u32[]{:S(2)}) copy-start(f32[1000]{0:T(1024)} %param.15) | copy-start | bytes 12004
  7.2 33.7 %copy-start.2 = (bf16[1,128,1280]{2,1,0:T(8,128)(2,1)S(1)}, bf16[1,128,1280]{2,1,0:T(8,128)(2,1)}, u32[]{:S(2)}) copy-start(bf16[1,128,1280]{2,1,0:T(8,128)(2,1)} %param.12) | copy-start | bytes 983044
  7.2 33.7 %copy-start.3 = (bf16[1,128,1280]{2,1,0:T(8,128)(2,1)S(1)}, bf16[1,128,1280]{2,1,0:T(8,128)(2,1)}, u32[]{:S(2)}) copy-start(bf16[1,128,1280]{2,1,0:T(8,128)(2,1)} %param.13) | copy-start | bytes 983044
  7.2 96.8 %copy-start.8 = (f32[1280]{0:T(1024)S(1)}, f32[1280]{0:T(1024)}, u32[]{:S(2)}) copy-start(f32[1280]{0:T(1024)} %param.17) | copy-start | bytes 15364
  7.2 96.8 %all-gather.5.cloned.1.call-start = ((), (), s32[]{:S(2)}) async-start(), calls=%async_computation.8 | async-start | bytes 10137600 | tf_op jit(solution)/shard_map/all_gather | solution.py:135
  38.4 203.2 %all-gather.7.cloned.1.call-start = ((), (), s32[]{:S(2)}) async-start(), calls=%async_computation.9 | async-start | bytes 5898240 | tf_op jit(solution)/shard_map/all_gather | solution.py:40
  42.0 68.3 %copy-start.7 = (bf16[40,160]{1,0:T(8,128)(2,1)S(1)}, bf16[40,160]{1,0:T(8,128)(2,1)}, u32[]{:S(2)}) copy-start(bf16[40,160]{1,0:T(8,128)(2,1)} %param.20) | copy-start | bytes 38404
  130.4 7.1 %copy-start.4 = (bf16[40,640]{1,0:T(8,128)(2,1)S(1)}, bf16[40,640]{1,0:T(8,128)(2,1)}, u32[]{:S(2)}) copy-start(bf16[40,640]{1,0:T(8,128)(2,1)} %param.22) | copy-start | bytes 153604
  130.4 7.1 %copy-start.5 = (bf16[40,640]{1,0:T(8,128)(2,1)S(1)}, bf16[40,640]{1,0:T(8,128)(2,1)}, u32[]{:S(2)}) copy-start(bf16[40,640]{1,0:T(8,128)(2,1)} %param.21) | copy-start | bytes 153604
  131.9 100.3 %all-to-all-start.2 = ((bf16[16,40,1280]{2,1,0:T(8,128)(2,1)}), bf16[16,40,1280]{2,1,0:T(8,128)(2,1)S(1)}, u32[]{:S(2)}, u32[]{:S(2)}) async-start(bf16[16,40,1280]{2,1,0:T(8,128)(2,1)} %broadcast_in_dim.30), calls=%async_computation.2 | async-start | bytes 3276800 | tf_op jit(solution)/shard_map/all_to_all | solution.py:18
  137.4 169.4 %all-gather.11.cloned.1.call-start = ((), (), s32[]{:S(2)}) async-start(), calls=%async_computation.11 | async-start | bytes 3379200 | tf_op jit(solution)/shard_map/all_gather | solution.py:40
  138.2 252.1 %all-gather.9.cloned.1.call-start = ((), (), s32[]{:S(2)}) async-start(), calls=%async_computation.10 | async-start | bytes 2949120 | tf_op jit(solution)/shard_map/all_gather | solution.py:153
  253.2 9.2 %copy-start.1 = (bf16[1,1024,1280]{1,2,0:T(8,128)(2,1)S(1)}, bf16[1,1024,1280]{1,2,0:T(8,128)(2,1)}, u32[]{:S(2)}) copy-start(bf16[1,1024,1280]{1,2,0:T(8,128)(2,1)} %copy.24) | copy-start | bytes 7864324
  262.4 6.2 %copy-start = (bf16[2,16,40,1280]{3,2,0,1:T(8,128)(2,1)S(1)}, bf16[2,16,40,1280]{3,2,0,1:T(8,128)(2,1)}, u32[]{:S(2)}) copy-start(bf16[2,16,40,1280]{3,2,0,1:T(8,128)(2,1)} %copy.28) | copy-start | bytes 9830404
  268.6 1.0 copy-start.9
  268.7 2.0 copy-start.6
  270.6 175.2 %reduce-scatter.3.cloned.1.call-start = ((), (), s32[]{:S(2)}) async-start(), calls=%async_computation.12 | async-start | bytes 3276800 | tf_op jit(solution)/shard_map/reduce_scatter | solution.py:54
  412.5 33.3 %copy-start.11 = (f32[1000]{0:T(1024)S(1)}, f32[1000]{0:T(1024)}, u32[]{:S(2)}) copy-start(f32[1000]{0:T(1024)} %param.16) | copy-start | bytes 12004
  412.5 67.0 %reduce-scatter.5.cloned.1.call-start = ((), (), s32[]{:S(2)}) async-start(), calls=%async_computation.13 | async-start | bytes 983040 | tf_op jit(solution)/shard_map/reduce_scatter | solution.py:54
Sparse Core Ops, SparseCore 0:
  38.5 65.4 all-gather.4
  110.3 98.7 all-gather.6
  211.0 93.0 all-gather.10
  307.1 83.1 all-gather.8
  412.6 33.1 reduce-scatter.2
  448.1 31.2 reduce-scatter.4
where the time goes:
time: 536 us
  waiting for transfers between devices  306 us (57%)
  blocking collectives  136 us (25%)
  matrix products  40.3 us (8%)
  local copies, waits for them, and re-layouts  23.1 us (4%)
  between operations  17.5 us (3%)
  other arithmetic  7.28 us (1%)
  starting transfers between devices  5.74 us (1%)
    all_to_all x1, waiting for transfers between devices, copy_for_each(): lax.all_to_all(jnp.broadcast_to(value[None], (length, *value.shape)), axi...  94 us
    all_to_all x5, blocking collectives, copy_for_each(): lax.all_to_all(jnp.broadcast_to(value[None], (length, *value.shape)), axi...  91.2 us
    all_gather x1, waiting for transfers between devices, shards(): ff_in = lax.all_gather(normed2, MP, axis=1, tiled=True)  83.4 us
    reduce_scatter x2, waiting for transfers between devices, sum_in_order(): blocks = lax.psum_scatter(blocks, axes[k], scatter_dimension=0, tiled=True)  66.2 us
    all_gather x1, waiting for transfers between devices, shards(): lax.all_gather(full_cols, DP, axis=1, tiled=True)  62 us
    psum x5, blocking collectives, by_axis(): value = lax.psum(value, axis)  44.8 us
    dot_general x1, matrix products, shards(): jnp.dot(hidden, whole_of(wdown, (('dp_0', 'dp_1'), 'dp_2'), 1), preferred...  12.9 us
    split x3, local copies, waits for them, and re-layouts, sent_together(): jnp.split(lax.all_gather(both, axis, axis=dim, tiled=True), ends, axis=al...  11.6 us
  transfers between devices with their start and end apart: 7, of which 5 were waited for; matrix products, arithmetic and copies ran while one was open for 7% of the time, Pallas kernels for 0%

commit v1 on v0

--- a/solution.py
+++ b/solution.py
@@ -150,7 +150,8 @@
         jnp.bfloat16
     )
     normed2 = layer_norm(resid, norm2_gain)
-    ff_in = lax.all_gather(normed2, MP, axis=1, tiled=True)
+    parts = lax.all_gather(normed2, MP, axis=0, tiled=False)
+    ff_in = jnp.concatenate(parts, axis=1)
     all_rows = ff_in.shape[1]
     ff_flat = ff_in.reshape(samples * all_rows, width)
     pieces = sent_together((wgate, wvalue), DP, 0, 1)

time: 536 us -> 536 us (level)
  no operation moved by 1% of the time
where the time goes in v1:
time: 536 us; the launch traced here: 535 us
  waiting for transfers between devices  306 us (57%)
  blocking collectives  136 us (25%)
  matrix products  40 us (7%)
  local copies, waits for them, and re-layouts  23.1 us (4%)
  between operations  17.5 us (3%)
  other arithmetic  7.28 us (1%)
  starting transfers between devices  5.74 us (1%)
    all_to_all x1, waiting for transfers between devices, copy_for_each(): lax.all_to_all(jnp.broadcast_to(value[None], (length, *value.shape)), axi...  94 us
    all_to_all x5, blocking collectives, copy_for_each(): lax.all_to_all(jnp.broadcast_to(value[None], (length, *value.shape)), axi...  91.2 us
    all_gather x1, waiting for transfers between devices, shards(): parts = lax.all_gather(normed2, MP, axis=0, tiled=False)  83.4 us
    reduce_scatter x2, waiting for transfers between devices, sum_in_order(): blocks = lax.psum_scatter(blocks, axes[k], scatter_dimension=0, tiled=True)  66.2 us
    all_gather x1, waiting for transfers between devices, shards(): lax.all_gather(full_cols, DP, axis=1, tiled=True)  62 us
    psum x5, blocking collectives, by_axis(): value = lax.psum(value, axis)  44.8 us
    dot_general x1, matrix products, shards(): jnp.dot(hidden, whole_of(wdown, (('dp_0', 'dp_1'), 'dp_2'), 1), preferred...  12.6 us
    split x3, local copies, waits for them, and re-layouts, sent_together(): jnp.split(lax.all_gather(both, axis, axis=dim, tiled=True), ends, axis=al...  11.6 us
  transfers between devices with their start and end apart: 7, of which 5 were waited for; matrix products, arithmetic and copies ran while one was open for 7% of the time, Pallas kernels for 0%

profile of v1, /device:TPU:32, one launch (start us, length us, event | category | flops | bytes accessed | tf_op | source)
XLA Modules:
  0.0 535.4 jit_solution(9544459507857209948)
XLA Ops:
  7.3 0.9 broadcast_in_dim.27
  8.2 28.9 %all_to_all.30 = bf16[8,3,40,160]{3,2,1,0:T(8,128)(2,1)S(1)} all-to-all(bf16[8,3,40,160]{3,2,1,0:T(8,128)(2,1)S(1)} %broadcast_in_dim.27), channel_id=1, replica_groups=mesh['dp_0'=4,'dp_1'=4,'dp_2'=2,'mp_0'=2,'mp_1'=4] {'mp_0','mp_1'}, dimensions={0} | all-to-all | bytes 614400 | tf_op jit(solution)/shard_map/all_to_all | solution.py:18
  37.2 1.2 reshape.149
  42.0 62.0 %all-gather.6.cloned.1.call-done = bf16[3,1280,1280]{2,1,0:T(8,128)(2,1)} async-done(((bf16[3,40,1280]{2,1,0:T(8,128)(2,1)}), bf16[3,1280,1280]{2,1,0:T(8,128)(2,1)}) %all-gather.6.cloned.1.call-update) | async-done | bytes 9830416 | tf_op jit(solution)/shard_map/all_gather | solution.py:135
  104.0 5.3 fusion.17
  110.2 20.1 %all_to_all.31 = bf16[8,40,160]{2,1,0:T(8,128)(2,1)S(1)} all-to-all(bf16[8,40,160]{2,1,0:T(8,128)(2,1)S(1)} %broadcast_in_dim.28), channel_id=1, replica_groups=mesh['dp_0'=4,'dp_1'=4,'dp_2'=2,'mp_0'=2,'mp_1'=4] {'mp_0','mp_1'}, dimensions={0} | all-to-all | bytes 204800 | tf_op jit(solution)/shard_map/all_to_all | solution.py:18
  130.6 1.3 broadcast_in_dim.30
  131.9 5.5 %all-to-all-start.2 = ((bf16[16,40,1280]{2,1,0:T(8,128)(2,1)}), bf16[16,40,1280]{2,1,0:T(8,128)(2,1)S(1)}, u32[]{:S(2)}, u32[]{:S(2)}) async-start(bf16[16,40,1280]{2,1,0:T(8,128)(2,1)} %broadcast_in_dim.30), calls=%async_computation.2 | async-start | bytes 3276800 | tf_op jit(solution)/shard_map/all_to_all | solution.py:18
  138.2 94.0 %all-to-all-done.2 = bf16[16,40,1280]{2,1,0:T(8,128)(2,1)S(1)} async-done(((bf16[16,40,1280]{2,1,0:T(8,128)(2,1)}), bf16[16,40,1280]{2,1,0:T(8,128)(2,1)S(1)}, u32[]{:S(2)}, u32[]{:S(2)}) %all-to-all-start.2) | async-done | bytes 1638432 | tf_op jit(solution)/shard_map/all_to_all | solution.py:18
  232.4 6.4 %all_to_all.32 = bf16[2,16,40,1280]{3,2,1,0:T(8,128)(2,1)S(1)} all-to-all(bf16[2,16,40,1280]{3,2,1,0:T(8,128)(2,1)S(1)} %broadcast_in_dim.31), channel_id=1, replica_groups=mesh['dp_0'=4,'dp_1'=4,'dp_2'=2,'mp_0'=2,'mp_1'=4] {'dp_2'}, dimensions={0} | all-to-all | bytes 6553600 | tf_op jit(solution)/shard_map/all_to_all | solution.py:18
  238.8 1.9 copy.28
  240.7 0.9 copy.25
  241.6 4.4 fusion.78
  246.0 4.5 copy.24
  250.5 2.7 copy.26
  253.2 9.2 %fusion.79 = (f32[20,128]{1,0:T(8,128)S(1)}, f32[20,128,1024]{2,1,0:T(8,128)}) fusion(bf16[128,20,64]{0,2,1:T(8,128)(2,1)} %bitcast.66, bf16[1024,20,64]{0,2,1:T(8,128)(2,1)} %bitcast.60), kind=kOutput, calls=%fused_computation.102 | convolution fusion | flops 343409664 | bytes 13445120 | tf_op jit(solution)/shard_map/while/body/eval_jaxpr/sub | solution.py:100
  262.4 6.2 %fusion.26 = bf16[20,64,128]{2,1,0:T(8,128)(2,1)S(1)} fusion(bf16[1024,20,64]{0,2,1:T(8,128)(2,1)S(1)} %bitcast.59, f32[20,128,1024]{2,1,0:T(8,128)} %get-tuple-element.24, f32[20,128]{1,0:T(8,128)S(1)} %get-tuple-element.23), kind=kOutput, calls=%fused_computation.37 | convolution fusion | flops 340951040 | bytes 13445120 | tf_op jit(solution)/shard_map/while/body/eval_jaxpr/hqk,khd->qhd/dot_general | solution.py:101
  269.7 0.9 multiply_convert_fusion
  270.7 30.8 %all_to_all.33 = bf16[16,640,40]{1,2,0:T(8,128)(2,1)S(1)} all-to-all(bf16[16,640,40]{1,2,0:T(8,128)(2,1)S(1)} %broadcast_in_dim.32), channel_id=1, replica_groups=mesh['dp_0'=4,'dp_1'=4,'dp_2'=2,'mp_0'=2,'mp_1'=4] {'dp_0','dp_1'}, dimensions={0} | all-to-all | bytes 1638400 | tf_op jit(solution)/shard_map/all_to_all | solution.py:18
  301.6 5.1 all_to_all.34
  306.8 83.4 %all-gather.12.cloned.1.call-done = bf16[8,128,1280]{2,1,0:T(8,128)(2,1)} async-done(((bf16[1,128,1280]{2,1,0:T(8,128)(2,1)}), bf16[8,128,1280]{2,1,0:T(8,128)(2,1)}) %all-gather.12.cloned.1.call-update) | async-done | bytes 2621456 | tf_op jit(solution)/shard_map/all_gather | solution.py:153
  390.2 5.9 %fusion.22 = f32[1024,640]{1,0:T(8,128)} fusion(bf16[1024,1280]{1,0:T(8,128)(2,1)} %bitcast.67, bf16[1280,1280]{1,0:T(8,128)(2,1)} %all-gather.10.cloned.1.call-done), kind=kOutput, calls=%fused_computation.35 | convolution fusion | flops 1677721600 | bytes 6881280 | tf_op jit(solution)/shard_map/dot_general | solution.py:159
  396.2 12.6 %convolution_convert_fusion = bf16[1024,1280]{1,0:T(8,128)(2,1)} fusion(bf16[640,1280]{0,1:T(8,128)(2,1)S(1)} %bitcast.63, f32[1024,640]{1,0:T(8,128)} %fusion.22, bf16[1024,1280]{1,0:T(8,128)(2,1)} %bitcast.68, bf16[1280,1280]{1,0:T(8,128)(2,1)} %all-gather.10.cloned.1.call-done), kind=kOutput, calls=%fused_computation.8 | convolution fusion | flops 3400007680 | bytes 11141120 | tf_op jit(solution)/shard_map/dot_general | solution.py:162
  408.7 3.4 copy.30
  412.2 33.2 %reduce-scatter.3.cloned.1.call-done = bf16[2,1,128,1280]{3,2,1,0:T(8,128)(2,1)} async-done(((bf16[8,1,128,1280]{3,2,1,0:T(8,128)(2,1)}), bf16[2,1,128,1280]{3,2,1,0:T(8,128)(2,1)}) %reduce-scatter.3.cloned.1.call-update) | async-done | bytes 655376 | tf_op jit(solution)/shard_map/reduce_scatter | solution.py:54
  446.2 33.0 %reduce-scatter.5.cloned.1.call-done = bf16[1,1,128,1280]{3,2,1,0:T(8,128)(2,1)} async-done(((bf16[2,1,128,1280]{3,2,1,0:T(8,128)(2,1)}), bf16[1,1,128,1280]{3,2,1,0:T(8,128)(2,1)}) %reduce-scatter.5.cloned.1.call-update) | async-done | bytes 327696 | tf_op jit(solution)/shard_map/reduce_scatter | solution.py:54
  479.1 3.2 fusion.37
  483.7 10.2 %psum.35 = f32[]{:T(128)} all-reduce(f32[]{:T(128)S(6)} %div.40), channel_id=1, replica_groups=mesh['dp_0'=4,'dp_1'=4,'dp_2'=2,'mp_0'=2,'mp_1'=4] {'dp_0'}, use_global_device_ids=true, to_apply=%region_11.12 | all-reduce | flops 1 | bytes 8 | tf_op jit(solution)/shard_map/psum | solution.py:70
  493.9 11.0 %psum.36 = f32[]{:T(128)} all-reduce(f32[]{:T(128)} %psum.35), channel_id=1, replica_groups=mesh['dp_0'=4,'dp_1'=4,'dp_2'=2,'mp_0'=2,'mp_1'=4] {'dp_1'}, use_global_device_ids=true, to_apply=%region_12.13 | all-reduce | flops 1 | bytes 8 | tf_op jit(solution)/shard_map/psum | solution.py:70
  504.9 3.1 psum.37
  508.0 9.4 %psum.38 = f32[]{:T(128)} all-reduce(f32[]{:T(128)} %psum.37), channel_id=1, replica_groups=mesh['dp_0'=4,'dp_1'=4,'dp_2'=2,'mp_0'=2,'mp_1'=4] {'mp_0'}, use_global_device_ids=true, to_apply=%region_14.15 | all-reduce | flops 1 | bytes 8 | tf_op jit(solution)/shard_map/psum | solution.py:70
  517.4 11.1 %psum.39 = f32[]{:T(128)} all-reduce(f32[]{:T(128)} %psum.38), channel_id=1, replica_groups=mesh['dp_0'=4,'dp_1'=4,'dp_2'=2,'mp_0'=2,'mp_1'=4] {'mp_1'}, use_global_device_ids=true, to_apply=%region_15.16 | all-reduce | flops 1 | bytes 8 | tf_op jit(solution)/shard_map/psum | solution.py:70
  (59 shorter events, 6.1 us)
Async XLA Ops:
  7.2 31.9 %copy-start.10 = (f32[1000]{0:T(1024)S(1)}, f32[1000]{0:T(1024)}, u32[]{:S(2)}) copy-start(f32[1000]{0:T(1024)} %param.15) | copy-start | bytes 12004
  7.2 33.7 %copy-start.2 = (bf16[1,128,1280]{2,1,0:T(8,128)(2,1)S(1)}, bf16[1,128,1280]{2,1,0:T(8,128)(2,1)}, u32[]{:S(2)}) copy-start(bf16[1,128,1280]{2,1,0:T(8,128)(2,1)} %param.12) | copy-start | bytes 983044
  7.2 33.7 %copy-start.3 = (bf16[1,128,1280]{2,1,0:T(8,128)(2,1)S(1)}, bf16[1,128,1280]{2,1,0:T(8,128)(2,1)}, u32[]{:S(2)}) copy-start(bf16[1,128,1280]{2,1,0:T(8,128)(2,1)} %param.13) | copy-start | bytes 983044
  7.2 96.8 %copy-start.8 = (f32[1280]{0:T(1024)S(1)}, f32[1280]{0:T(1024)}, u32[]{:S(2)}) copy-start(f32[1280]{0:T(1024)} %param.17) | copy-start | bytes 15364
  7.2 96.8 %all-gather.6.cloned.1.call-start = ((), (), s32[]{:S(2)}) async-start(), calls=%async_computation.8 | async-start | bytes 10137600 | tf_op jit(solution)/shard_map/all_gather | solution.py:135
  38.4 203.2 %all-gather.8.cloned.1.call-start = ((), (), s32[]{:S(2)}) async-start(), calls=%async_computation.9 | async-start | bytes 5898240 | tf_op jit(solution)/shard_map/all_gather | solution.py:40
  42.0 68.3 %copy-start.7 = (bf16[40,160]{1,0:T(8,128)(2,1)S(1)}, bf16[40,160]{1,0:T(8,128)(2,1)}, u32[]{:S(2)}) copy-start(bf16[40,160]{1,0:T(8,128)(2,1)} %param.20) | copy-start | bytes 38404
  130.4 7.1 %copy-start.4 = (bf16[40,640]{1,0:T(8,128)(2,1)S(1)}, bf16[40,640]{1,0:T(8,128)(2,1)}, u32[]{:S(2)}) copy-start(bf16[40,640]{1,0:T(8,128)(2,1)} %param.22) | copy-start | bytes 153604
  130.4 7.1 %copy-start.5 = (bf16[40,640]{1,0:T(8,128)(2,1)S(1)}, bf16[40,640]{1,0:T(8,128)(2,1)}, u32[]{:S(2)}) copy-start(bf16[40,640]{1,0:T(8,128)(2,1)} %param.21) | copy-start | bytes 153604
  131.9 100.3 %all-to-all-start.2 = ((bf16[16,40,1280]{2,1,0:T(8,128)(2,1)}), bf16[16,40,1280]{2,1,0:T(8,128)(2,1)S(1)}, u32[]{:S(2)}, u32[]{:S(2)}) async-start(bf16[16,40,1280]{2,1,0:T(8,128)(2,1)} %broadcast_in_dim.30), calls=%async_computation.2 | async-start | bytes 3276800 | tf_op jit(solution)/shard_map/all_to_all | solution.py:18
  137.4 169.4 %all-gather.10.cloned.1.call-start = ((), (), s32[]{:S(2)}) async-start(), calls=%async_computation.10 | async-start | bytes 3379200 | tf_op jit(solution)/shard_map/all_gather | solution.py:40
  138.2 252.1 %all-gather.12.cloned.1.call-start = ((), (), s32[]{:S(2)}) async-start(), calls=%async_computation.13 | async-start | bytes 2949120 | tf_op jit(solution)/shard_map/all_gather | solution.py:153
  253.2 9.2 %copy-start.1 = (bf16[1,1024,1280]{1,2,0:T(8,128)(2,1)S(1)}, bf16[1,1024,1280]{1,2,0:T(8,128)(2,1)}, u32[]{:S(2)}) copy-start(bf16[1,1024,1280]{1,2,0:T(8,128)(2,1)} %copy.24) | copy-start | bytes 7864324
  262.4 6.2 %copy-start = (bf16[2,16,40,1280]{3,2,0,1:T(8,128)(2,1)S(1)}, bf16[2,16,40,1280]{3,2,0,1:T(8,128)(2,1)}, u32[]{:S(2)}) copy-start(bf16[2,16,40,1280]{3,2,0,1:T(8,128)(2,1)} %copy.28) | copy-start | bytes 9830404
  268.6 1.0 copy-start.9
  268.7 2.0 copy-start.6
  270.6 174.9 %reduce-scatter.3.cloned.1.call-start = ((), (), s32[]{:S(2)}) async-start(), calls=%async_computation.11 | async-start | bytes 3276800 | tf_op jit(solution)/shard_map/reduce_scatter | solution.py:54
  412.2 33.3 %copy-start.11 = (f32[1000]{0:T(1024)S(1)}, f32[1000]{0:T(1024)}, u32[]{:S(2)}) copy-start(f32[1000]{0:T(1024)} %param.16) | copy-start | bytes 12004
  412.2 67.0 %reduce-scatter.5.cloned.1.call-start = ((), (), s32[]{:S(2)}) async-start(), calls=%async_computation.12 | async-start | bytes 983040 | tf_op jit(solution)/shard_map/reduce_scatter | solution.py:54
Sparse Core Ops, SparseCore 0:
  38.5 65.4 all-gather.5
  110.3 98.7 all-gather.7
  211.0 93.0 all-gather.9
  307.1 83.1 all-gather.11
  412.3 33.1 reduce-scatter.2
  447.8 31.2 reduce-scatter.4
